TPU v7x, 256 devices: a whole 4x4x8 slice. The times are simulated.
256 devices in a mesh: dp: 8 (over z_lo, x), ctx: 32 (over z_hi, y, core).
Axes of the slice: x: 4, y: 4, z: 8 (z_hi: 4, z_lo: 2; z = z_hi * 2 + z_lo), core: 2. Of those that a mesh axis runs over, the one named last changes fastest.
Arguments:
- tokens: bfloat16 [8, 4096, 4096], P('dp', 'ctx'), may hold values from -6 to 6
- proj_weight: bfloat16 [4096, 512], P('dp'), may hold values from -0.09375 to 0.09375
- values: bfloat16 [8, 4096, 2048], P('dp', 'ctx'), may hold values from -60 to 60
- grad_out: bfloat16 [8, 4096, 2048], P('dp', 'ctx'), may hold values from -6 to 6
Outputs:
- attended: bfloat16 [8, 4096, 2048], P('dp', 'ctx')
- grad_tokens: bfloat16 [8, 4096, 4096], P('dp', 'ctx')
- grad_values: bfloat16 [8, 4096, 2048], P('dp', 'ctx')
- grad_proj: float32 [4096, 512], P(('dp', 'ctx'))
All inputs are finite; a program needn't handle non-finite values.
Results may differ from a plain program's by a relative error of at most 0.0049.
Values may be sent and summed in bfloat16 or wider, within the bound.
A program may use at most 192 MiB of HBM per device.

v0:
```python
import jax
import jax.numpy as jnp
from jax import lax
from jax.sharding import PartitionSpec as P

H = 16
F = 16
DH = 128
HIGHEST = lax.Precision.HIGHEST
QUAD_SCALE = 0.17677669529663687
EPSILON = 1e-05


def features(inputs):
    count_heads, count_rows, count_feat = inputs.shape
    linear = jnp.swapaxes(inputs, 1, 2) * 0.5
    square = (inputs[:, :, :, None] * inputs[:, :, None, :]).reshape(
        count_heads, count_rows, count_feat * count_feat
    )
    square = jnp.swapaxes(square, 1, 2) * QUAD_SCALE
    constant_row = jnp.ones((count_heads, 1, count_rows), inputs.dtype)
    return jnp.concatenate([constant_row, linear, square], axis=1)


def block_kernel(query_part, key_part):
    count_rows = query_part.shape[1]
    causal = lax.broadcasted_iota(jnp.int32, (count_rows, count_rows), 0) >= lax.broadcasted_iota(
        jnp.int32, (count_rows, count_rows), 1
    )
    scores = jnp.einsum("htf,hsf->hts", query_part, key_part, precision=HIGHEST) * 0.25
    kernel = jnp.where(causal, 1.0 + scores + 0.5 * scores * scores, 0.0)
    return (causal, scores, kernel)


def normalize(numerator):
    inv_rms = lax.rsqrt(jnp.mean(numerator * numerator, axis=-1, keepdims=True) + EPSILON)
    return (inv_rms, numerator * inv_rms)


def grad_normalize(inv_rms, normed, upstream):
    return inv_rms * (upstream - normed * jnp.mean(normed * upstream, axis=-1, keepdims=True))


def local_backward(
    query_part,
    key_part,
    value_part,
    grad_num,
    causal,
    scores,
    kernel,
    pull_query,
    pull_key,
    feat_key,
    prefix,
    suffix,
):
    mixing = jnp.where(
        causal, jnp.einsum("htd,hsd->hts", grad_num, value_part, precision=HIGHEST), 0.0
    )
    slope = mixing * (1.0 + scores)
    grad_query = jnp.einsum("hts,hsf->htf", slope, key_part, precision=HIGHEST) * 0.25
    grad_key = jnp.einsum("hts,htf->hsf", slope, query_part, precision=HIGHEST) * 0.25
    grad_query = (
        grad_query + pull_query(jnp.einsum("hed,htd->het", prefix, grad_num, precision=HIGHEST))[0]
    )
    grad_key = (
        grad_key + pull_key(jnp.einsum("hed,htd->het", suffix, value_part, precision=HIGHEST))[0]
    )
    grad_value = jnp.einsum("hts,htd->hsd", kernel, grad_num, precision=HIGHEST)
    grad_value = grad_value + jnp.einsum("het,hed->htd", feat_key, suffix, precision=HIGHEST)
    return (grad_query, grad_key, grad_value)


def exclusive(blocks, later):
    count = blocks.shape[0]
    row = lax.broadcasted_iota(jnp.int32, (count, count), 0)
    col = lax.broadcasted_iota(jnp.int32, (count, count), 1)
    chosen = col > row if later else col < row
    return jnp.dot(chosen.astype(jnp.float32), blocks, precision=HIGHEST)


def split_heads(matrix, size):
    return jnp.swapaxes(matrix.reshape(matrix.shape[0], -1, size), 0, 1)


def merge_heads(blocked):
    return jnp.swapaxes(blocked, 0, 1).reshape(blocked.shape[1], -1)


def local(tokens, proj_weight, values, grad_out):
    token_rows = tokens[0]
    query_cols = H * F
    tokens_cols = lax.all_to_all(token_rows, "dp", split_axis=1, concat_axis=0, tiled=True)
    projected = jnp.dot(
        token_rows,
        lax.all_gather(proj_weight, "dp", axis=0, tiled=True),
        preferred_element_type=jnp.float32,
    )
    query_part = split_heads(projected[:, :query_cols], F)
    key_part = split_heads(projected[:, query_cols:], F)
    value_part = split_heads(values[0].astype(jnp.float32), DH)
    upstream = split_heads(grad_out[0].astype(jnp.float32), DH)
    feat_query, pull_query = jax.vjp(features, query_part)
    feat_key, pull_key = jax.vjp(features, key_part)
    local_term = jnp.einsum("het,htd->hed", feat_key, value_part, precision=HIGHEST)
    columns_in = lax.all_to_all(
        local_term.reshape(1, -1), "ctx", split_axis=1, concat_axis=0, tiled=True
    )
    running = exclusive(columns_in, False)
    prefix = lax.all_to_all(running, "ctx", split_axis=0, concat_axis=1, tiled=True).reshape(
        local_term.shape
    )
    causal, scores, kernel = block_kernel(query_part, key_part)
    numerator = jnp.einsum("hts,hsd->htd", kernel, value_part, precision=HIGHEST)
    numerator = numerator + jnp.einsum("het,hed->htd", feat_query, prefix, precision=HIGHEST)
    inv_rms, normed = normalize(numerator)
    attended = merge_heads(normed).astype(jnp.bfloat16)
    grad_num = grad_normalize(inv_rms, normed, upstream)
    carried = jnp.einsum("het,htd->hed", feat_query, grad_num, precision=HIGHEST)
    later_in = lax.all_to_all(
        carried.reshape(1, -1), "ctx", split_axis=1, concat_axis=0, tiled=True
    )
    later_running = exclusive(later_in, True)
    suffix = lax.all_to_all(later_running, "ctx", split_axis=0, concat_axis=1, tiled=True).reshape(
        carried.shape
    )
    grad_query, grad_key, grad_value = local_backward(
        query_part,
        key_part,
        value_part,
        grad_num,
        causal,
        scores,
        kernel,
        pull_query,
        pull_key,
        feat_key,
        prefix,
        suffix,
    )
    grad_proj_rows = jnp.concatenate(
        [merge_heads(grad_query), merge_heads(grad_key)], axis=1
    ).astype(jnp.bfloat16)
    grad_tokens = lax.dot_general(
        grad_proj_rows,
        lax.all_gather(proj_weight, "dp", axis=0, tiled=True),
        (((1,), (1,)), ((), ())),
        preferred_element_type=jnp.float32,
    ).astype(jnp.bfloat16)
    rows_all = lax.all_gather(grad_proj_rows, "dp", axis=0, tiled=True)
    grad_proj = lax.psum_scatter(
        lax.dot_general(
            tokens_cols, rows_all, (((0,), (0,)), ((), ())), preferred_element_type=jnp.float32
        ),
        "ctx",
        scatter_dimension=0,
        tiled=True,
    )
    grad_values = merge_heads(grad_value).astype(jnp.bfloat16)
    return (attended[None], grad_tokens[None], grad_values[None], grad_proj)


def solution(mesh):
    return jax.shard_map(
        local,
        mesh=mesh,
        in_specs=(P("dp", "ctx", None), P("dp", None), P("dp", "ctx", None), P("dp", "ctx", None)),
        out_specs=(
            P("dp", "ctx", None),
            P("dp", "ctx", None),
            P("dp", "ctx", None),
            P(("dp", "ctx"), None),
        ),
        check_vma=False,
    )
```

profile of v0, /device:TPU:2, one launch (start us, length us, event | category | flops | bytes accessed | tf_op | source)
XLA Modules:
  0.0 523.0 jit_solution(1464538950625554450)
XLA Ops:
  7.9 1.1 copy.72
  9.1 56.6 %all-gather.3.cloned.1.call-done = bf16[4096,512]{1,0:T(8,128)(2,1)} async-done(((bf16[512,512]{1,0:T(8,128)(2,1)}), bf16[4096,512]{1,0:T(8,128)(2,1)}) %all-gather.3.cloned.1.call-update) | async-done | bytes 4194320 | tf_op jit(solution)/shard_map/all_gather | solution.py:97
  65.7 3.2 fusion.22
  69.4 1.4 copy-done.1
  70.8 2.1 fusion.6
  72.9 3.7 all_to_all.72
  76.6 65.7 %all_to_all.79 = f32[1,32,17472]{2,0,1:T(1,128)S(1)} all-to-all(f32[1,32,17472]{2,0,1:T(1,128)} %all_to_all.72), channel_id=1, replica_groups=mesh['dp'=8,'ctx'=32] {'ctx'}, dimensions={1} | all-to-all | bytes 4472832 | tf_op jit(solution)/shard_map/all_to_all | solution.py:107
  142.3 1.2 convolution_bitcast_fusion.1
  143.5 3.7 copy.50
  147.2 4.5 all-to-all-start.1
  151.8 1.2 copy.51
  153.8 2.7 fusion.60
  156.5 2.9 multiply_multiply_fusion.1
  159.5 46.6 %all-to-all-done.1 = f32[32,1,17472]{2,1,0:T(1,128)S(1)} async-done(((f32[32,1,17472]{2,1,0:T(1,128)}), f32[32,1,17472]{2,1,0:T(1,128)S(1)}, u32[]{:S(2)}, u32[]{:S(2)}) %all-to-all-start.1) | async-done | bytes 2236448 | tf_op jit(solution)/shard_map/all_to_all | solution.py:111
  206.0 7.3 %reduce = f32[32,17472]{1,0:T(8,128)} reduce(f32[32,1,17472]{2,1,0:T(1,128)S(1)} %all-to-all-done.1, f32[]{:T(128)} %constant.24), dimensions={1}, to_apply=%all_to_all.62.reduce_sub_computation | reduce | bytes 4472836 | tf_op jit(solution)/shard_map/all_to_all | solution.py:111
  213.3 2.4 reshape.143
  215.8 6.9 %fusion.8 = f32[16,128,128]{1,2,0:T(8,128)S(1)} fusion(f32[16,273,128]{2,1,0:T(8,128)S(1)} %reshape.143, f32[16,256,128]{2,1,0:T(8,128)} %bitcast.119, f32[16,16,128]{2,1,0:T(8,128)} %multiply_bitcast_fusion.1, f32[273]{0:T(512)S(1)} %pad.5.clone), kind=kOutput, calls=%fused_computation.21 | convolution fusion | flops 859901952 | bytes 5514308 | tf_op jit(solution)/shard_map/het,hed->htd/dot_general | solution.py:116
  222.8 1.4 multiply_reduce_fusion.5
  225.3 1.1 copy-done
  226.4 5.3 %fusion.7 = f32[16,273,128]{2,1,0:T(8,128)} fusion(f32[16,128,128]{1,2,0:T(8,128)S(1)} %subtract_multiply_fusion, f32[16,256,128]{2,1,0:T(8,128)S(1)} %bitcast.120, f32[16,16,128]{2,1,0:T(8,128)S(1)} %copy-done.17, f32[273]{0:T(512)S(1)} %pad.5.clone), kind=kOutput, calls=%fused_computation.20 | convolution fusion | flops 859901952 | bytes 5514308 | tf_op jit(solution)/shard_map/het,htd->hed/dot_general | solution.py:120
  231.7 5.2 all_to_all.73
  236.9 58.5 %all_to_all.80 = f32[1,32,17472]{2,0,1:T(1,128)S(1)} all-to-all(f32[1,32,17472]{2,0,1:T(1,128)} %all_to_all.73), channel_id=1, replica_groups=mesh['dp'=8,'ctx'=32] {'ctx'}, dimensions={1} | all-to-all | bytes 4472832 | tf_op jit(solution)/shard_map/all_to_all | solution.py:121
  295.4 1.2 convolution_bitcast_fusion
  296.6 3.8 copy.56
  300.3 5.8 %all-to-all-start.3 = ((f32[32,1,17472]{2,1,0:T(1,128)}), f32[32,1,17472]{2,1,0:T(1,128)}, u32[]{:S(2)}, u32[]{:S(2)}) async-start(f32[32,1,17472]{2,1,0:T(1,128)} %copy.56), calls=%async_computation.3 | async-start | bytes 4489216 | tf_op jit(solution)/shard_map/all_to_all | solution.py:125
  306.1 2.3 copy.57
  308.4 3.9 fusion.61
  313.2 1.0 multiply_reduce_fusion.2
  314.5 1.0 fusion.9
  316.6 1.7 fusion.20
  318.3 40.6 %all-to-all-done.3 = f32[32,1,17472]{2,1,0:T(1,128)} async-done(((f32[32,1,17472]{2,1,0:T(1,128)}), f32[32,1,17472]{2,1,0:T(1,128)}, u32[]{:S(2)}, u32[]{:S(2)}) %all-to-all-start.3) | async-done | bytes 2236448 | tf_op jit(solution)/shard_map/all_to_all | solution.py:125
  358.9 7.7 %all-to-all-start.4 = ((bf16[128,8,512]{0,2,1:T(8,128)(2,1)}), bf16[128,8,512]{0,2,1:T(8,128)(2,1)}, u32[]{:S(2)}, u32[]{:S(2)}) async-start(bf16[128,8,512]{0,2,1:T(8,128)(2,1)} %bitcast.40), calls=%async_computation.4 | async-start | bytes 2097152 | tf_op jit(solution)/shard_map/all_to_all | solution.py:94
  366.8 8.4 %reduce.1 = f32[32,17472]{1,0:T(8,128)} reduce(f32[32,1,17472]{2,1,0:T(1,128)} %all-to-all-done.3, f32[]{:T(128)} %constant.24), dimensions={1}, to_apply=%all_to_all.67.reduce_sub_computation | reduce | bytes 4472836 | tf_op jit(solution)/shard_map/all_to_all | solution.py:125
  375.3 2.2 reshape.146
  377.5 3.1 fusion.27
  380.8 1.1 multiply_reduce_fusion
  382.0 1.0 fusion.19
  384.1 2.3 copy.58
  386.3 32.8 %all-gather.5.cloned.1.call-done = bf16[1024,512]{0,1:T(8,128)(2,1)} async-done(((bf16[128,512]{0,1:T(8,128)(2,1)}), bf16[1024,512]{0,1:T(8,128)(2,1)}) %all-gather.5.cloned.1.call-update) | async-done | bytes 1048592 | tf_op jit(solution)/shard_map/all_gather | solution.py:151
  419.1 3.3 convolution_bitcast_fusion.2
  422.4 2.5 copy.68
  424.9 2.2 fusion.21
  427.1 2.0 copy.59
  429.1 7.0 %fusion.5 = f32[16,128,128]{1,2,0:T(8,128)S(1)} fusion(f32[16,273,128]{2,1,0:T(8,128)S(1)} %reshape.146, f32[16,256,128]{2,1,0:T(8,128)} %bitcast.122, f32[16,16,128]{2,1,0:T(8,128)S(1)} %copy-done.16, f32[273]{0:T(512)} %copy-done.21), kind=kOutput, calls=%fused_computation.18 | convolution fusion | flops 859901952 | bytes 5514308 | tf_op jit(solution)/shard_map/het,hed->htd/dot_general | solution.py:71
  436.1 1.4 fusion.10
  437.5 1.0 copy.60
  438.5 4.7 fusion
  443.2 72.8 %reduce-scatter.4.cloned.1.call-done = f32[16,512]{1,0:T(8,128)} async-done(((f32[512,512]{1,0:T(8,128)}), f32[16,512]{1,0:T(8,128)}) %reduce-scatter.4.cloned.1.call-update) | async-done | bytes 32784
  (64 shorter events, 7.0 us)
Async XLA Ops:
  7.2 58.6 %all-gather.3.cloned.1.call-start = ((), (), s32[]{:S(2)}) async-start(), calls=%async_computation.6 | async-start | bytes 4718592 | tf_op jit(solution)/shard_map/all_gather | solution.py:97
  9.1 60.3 %copy-start.6 = (bf16[16,8,16,128]{3,2,1,0:T(8,128)(2,1)}, bf16[16,8,16,128]{3,2,1,0:T(8,128)(2,1)S(1)}, u32[]{:S(2)}) copy-start(bf16[16,8,16,128]{3,2,1,0:T(8,128)(2,1)S(1)} %copy.72) | copy-start | bytes 1572868
  9.1 216.3 %copy-start.21 = (f32[273]{0:T(512)}, f32[273]{0:T(512)S(1)}, u32[]{:S(2)}) copy-start(f32[273]{0:T(512)S(1)} %pad.5.clone) | copy-start | bytes 3280
  69.1 3.8 copy-start.15
  69.4 1.4 copy-start.1
  147.2 4.6 copy-start.20
  147.2 58.8 %all-to-all-start.1 = ((f32[32,1,17472]{2,1,0:T(1,128)}), f32[32,1,17472]{2,1,0:T(1,128)S(1)}, u32[]{:S(2)}, u32[]{:S(2)}) async-start(f32[32,1,17472]{2,1,0:T(1,128)} %copy.50), calls=%async_computation.1 | async-start | bytes 4489216 | tf_op jit(solution)/shard_map/all_to_all | solution.py:111
  153.1 0.7 copy-start.12
  156.5 66.2 %copy-start.2 = (f32[16,128,128]{2,1,0:T(8,128)}, f32[16,128,128]{2,1,0:T(8,128)S(1)}, u32[]{:S(2)}) copy-start(f32[16,128,128]{2,1,0:T(8,128)S(1)} %fusion.60) | copy-start | bytes 3145732
  215.8 7.0 %copy-start.7 = (bf16[16,8,16,128]{3,2,1,0:T(8,128)(2,1)S(1)}, bf16[16,8,16,128]{3,2,1,0:T(8,128)(2,1)}, u32[]{:S(2)}) copy-start(bf16[16,8,16,128]{3,2,1,0:T(8,128)(2,1)} %copy-done.6) | copy-start | bytes 1572868
  222.7 2.1 copy-start.11
  224.1 1.0 copy-start.5
  224.8 1.6 copy-start
  224.8 1.6 copy-start.17
  300.3 58.6 %all-to-all-start.3 = ((f32[32,1,17472]{2,1,0:T(1,128)}), f32[32,1,17472]{2,1,0:T(1,128)}, u32[]{:S(2)}, u32[]{:S(2)}) async-start(f32[32,1,17472]{2,1,0:T(1,128)} %copy.56), calls=%async_computation.3 | async-start | bytes 4489216 | tf_op jit(solution)/shard_map/all_to_all | solution.py:125
  312.3 0.9 copy-start.13
  313.2 1.2 copy-start.3
  313.2 1.4 copy-start.8
  315.6 1.0 copy-start.9
  358.9 25.1 %all-to-all-start.4 = ((bf16[128,8,512]{0,2,1:T(8,128)(2,1)}), bf16[128,8,512]{0,2,1:T(8,128)(2,1)}, u32[]{:S(2)}, u32[]{:S(2)}) async-start(bf16[128,8,512]{0,2,1:T(8,128)(2,1)} %bitcast.40), calls=%async_computation.4 | async-start | bytes 2097152 | tf_op jit(solution)/shard_map/all_to_all | solution.py:94
  366.6 52.5 %all-gather.5.cloned.1.call-start = ((), (), s32[]{:S(2)}) async-start(), calls=%async_computation.7 | async-start | bytes 1179648 | tf_op jit(solution)/shard_map/all_gather | solution.py:151
  380.8 1.2 copy-start.10
  380.8 1.2 copy-start.14
  383.0 39.3 %copy-start.18 = (bf16[128,16,16]{0,2,1:T(8,128)(2,1)}, bf16[128,16,16]{0,2,1:T(8,128)(2,1)S(1)}, u32[]{:S(2)}) copy-start(bf16[128,16,16]{0,2,1:T(8,128)(2,1)S(1)} %fusion.19) | copy-start | bytes 196612
  383.7 132.2 %reduce-scatter.4.cloned.1.call-start = ((), (), s32[]{:S(2)}) async-start(), calls=%async_computation.8 | async-start | bytes 1081344
  424.9 4.2 copy-start.16
  429.1 7.0 %copy-start.4 = (f32[16,128,128]{2,1,0:T(8,128)S(1)}, f32[16,128,128]{2,1,0:T(8,128)}, u32[]{:S(2)}) copy-start(f32[16,128,128]{2,1,0:T(8,128)} %copy-done.2) | copy-start | bytes 3145732
  436.1 2.4 copy-start.19
Sparse Core Ops, SparseCore 0:
  9.8 55.8 all-gather.2
  383.9 35.1 all-gather.4
  425.0 90.9 reduce-scatter.3
where the time goes:
time: 531 us; the launch traced here: 523 us
  waiting for transfers between devices  250 us (47%)
  blocking collectives  124 us (23%)
  matrix products  50.9 us (10%)
  local copies, waits for them, and re-layouts  38.5 us (7%)
  other arithmetic  26.1 us (5%)
  starting transfers between devices  18.6 us (4%)
  between operations  14.6 us (3%)
    unnamed x4, waiting for transfers between devices  73.5 us
    all_to_all x1, blocking collectives, local(): lax.all_to_all(local_term.reshape(1, -1), 'ctx', split_axis=1, concat_axi...  65.7 us
    all_to_all x1, blocking collectives, local(): lax.all_to_all(carried.reshape(1, -1), 'ctx', split_axis=1, concat_axis=0...  58.5 us
    all_gather x1, waiting for transfers between devices, local(): lax.all_gather(proj_weight, 'dp', axis=0, tiled=True)  56.6 us
    all_to_all x1, waiting for transfers between devices, local(): lax.all_to_all(running, 'ctx', split_axis=0, concat_axis=1, tiled=True)  46.6 us
    all_to_all x1, waiting for transfers between devices, local(): lax.all_to_all(later_running, 'ctx', split_axis=0, concat_axis=1, tiled=T...  40.6 us
    all_gather x1, waiting for transfers between devices, local(): rows_all = lax.all_gather(grad_proj_rows, 'dp', axis=0, tiled=True)  32.8 us
    unnamed x49, local copies, waits for them, and re-layouts  13.7 us
  transfers between devices with their start and end apart: 6, of which 5 were waited for; matrix products, arithmetic and copies ran while one was open for 11% of the time, Pallas kernels for 0%

commit v1 on v0

--- a/solution.py
+++ b/solution.py
@@ -104,8 +104,14 @@
     feat_query, pull_query = jax.vjp(features, query_part)
     feat_key, pull_key = jax.vjp(features, key_part)
     local_term = jnp.einsum("het,htd->hed", feat_key, value_part, precision=HIGHEST)
-    columns_in = lax.all_to_all(
-        local_term.reshape(1, -1), "ctx", split_axis=1, concat_axis=0, tiled=True
+    columns_in = jnp.concatenate(
+        lax.all_to_all(
+            jnp.stack(jnp.split(local_term.reshape(1, -1), lax.axis_size("ctx"), axis=1)),
+            "ctx",
+            0,
+            0,
+        ),
+        axis=0,
     )
     running = exclusive(columns_in, False)
     prefix = lax.all_to_all(running, "ctx", split_axis=0, concat_axis=1, tiled=True).reshape(

time: 531 us -> 550 us (1.036)
  local copies, waits for them, and re-layouts: 38.5 us -> 57.1 us
    unnamed x49 -> x84, local copies, waits for them, and re-layouts: 13.7 us -> 31.8 us
  transfers between devices with their start and end apart: 6 -> 6, of which waited for: 5 -> 5; matrix products, arithmetic and copies ran while one was open for 11% -> 10% of each run, Pallas kernels for 0% -> 0%
where the time goes in v1:
time: 550 us; the launch traced here: 543 us
  waiting for transfers between devices  252 us (46%)
  blocking collectives  127 us (23%)
  local copies, waits for them, and re-layouts  57.1 us (10%)
  matrix products  50.9 us (9%)
  other arithmetic  26.2 us (5%)
  starting transfers between devices  15 us (3%)
  between operations  14.7 us (3%)
    unnamed x4, waiting for transfers between devices  73.5 us
    all_to_all x1, blocking collectives, local(): lax.all_to_all(jnp.stack(jnp.split(local_term.reshape(1, -1), lax.axis_si...  65.8 us
    all_to_all x1, blocking collectives, local(): lax.all_to_all(carried.reshape(1, -1), 'ctx', split_axis=1, concat_axis=0...  61.2 us
    all_gather x1, waiting for transfers between devices, local(): lax.all_gather(proj_weight, 'dp', axis=0, tiled=True)  56.6 us
    all_to_all x1, waiting for transfers between devices, local(): lax.all_to_all(running, 'ctx', split_axis=0, concat_axis=1, tiled=True)  46.2 us
    all_to_all x1, waiting for transfers between devices, local(): lax.all_to_all(later_running, 'ctx', split_axis=0, concat_axis=1, tiled=T...  41.6 us
    all_gather x1, waiting for transfers between devices, local(): rows_all = lax.all_gather(grad_proj_rows, 'dp', axis=0, tiled=True)  33.7 us
    unnamed x84, local copies, waits for them, and re-layouts  31.8 us
  transfers between devices with their start and end apart: 6, of which 5 were waited for; matrix products, arithmetic and copies ran while one was open for 10% of the time, Pallas kernels for 0%

profile of v1, /device:TPU:2, one launch (start us, length us, event | category | flops | bytes accessed | tf_op | source)
XLA Modules:
  0.0 542.6 jit_solution(13795907868776219452)
XLA Ops:
  7.9 1.1 copy.71
  9.1 56.6 %all-gather.3.cloned.1.call-done = bf16[4096,512]{1,0:T(8,128)(2,1)} async-done(((bf16[512,512]{1,0:T(8,128)(2,1)}), bf16[4096,512]{1,0:T(8,128)(2,1)}) %all-gather.3.cloned.1.call-update) | async-done | bytes 4194320 | tf_op jit(solution)/shard_map/all_gather | solution.py:97
  65.7 3.2 fusion.22
  70.1 1.3 copy-done.1
  71.4 2.1 fusion.6
  73.5 3.6 reshape.141
  80.1 1.1 fusion.74
  82.2 1.1 fusion.72
  84.2 1.1 fusion.70
  86.2 1.1 fusion.68
  88.2 1.1 fusion.66
  92.3 1.1 fusion.62
  95.5 65.8 %all_to_all.67 = f32[32,1,17472]{2,1,0:T(1,128)S(1)} all-to-all(f32[32,1,17472]{2,1,0:T(1,128)S(1)} %fusion.46), channel_id=1, replica_groups=mesh['dp'=8,'ctx'=32] {'ctx'}, dimensions={0} | all-to-all | bytes 4472832 | tf_op jit(solution)/shard_map/all_to_all | solution.py:108
  161.3 1.2 convolution_bitcast_fusion.1
  162.5 3.7 copy.49
  166.2 4.3 all-to-all-start.1
  170.6 1.2 copy.50
  172.6 2.7 fusion.92
  175.3 2.9 multiply_multiply_fusion.1
  178.3 46.2 %all-to-all-done.1 = f32[32,1,17472]{2,1,0:T(1,128)S(1)} async-done(((f32[32,1,17472]{2,1,0:T(1,128)}), f32[32,1,17472]{2,1,0:T(1,128)S(1)}, u32[]{:S(2)}, u32[]{:S(2)}) %all-to-all-start.1) | async-done | bytes 2236448 | tf_op jit(solution)/shard_map/all_to_all | solution.py:117
  224.4 7.3 %reduce = f32[32,17472]{1,0:T(8,128)} reduce(f32[32,1,17472]{2,1,0:T(1,128)S(1)} %all-to-all-done.1, f32[]{:T(128)} %constant.24), dimensions={1}, to_apply=%all_to_all.51.reduce_sub_computation | reduce | bytes 4472836 | tf_op jit(solution)/shard_map/all_to_all | solution.py:117
  231.8 2.6 reshape.143
  234.4 6.9 %fusion.8 = f32[16,128,128]{1,2,0:T(8,128)S(1)} fusion(f32[16,273,128]{2,1,0:T(8,128)S(1)} %reshape.143, f32[16,256,128]{2,1,0:T(8,128)} %bitcast.247, f32[16,16,128]{2,1,0:T(8,128)} %multiply_bitcast_fusion.1, f32[273]{0:T(512)S(1)} %pad.5.clone), kind=kOutput, calls=%fused_computation.21 | convolution fusion | flops 859901952 | bytes 5514308 | tf_op jit(solution)/shard_map/het,hed->htd/dot_general | solution.py:122
  241.4 1.4 multiply_reduce_fusion.5
  245.0 5.3 fusion.7
  250.3 4.9 all_to_all.61
  255.2 61.2 %all_to_all.68 = f32[1,32,17472]{2,0,1:T(1,128)S(1)} all-to-all(f32[1,32,17472]{2,0,1:T(1,128)} %all_to_all.61), channel_id=1, replica_groups=mesh['dp'=8,'ctx'=32] {'ctx'}, dimensions={1} | all-to-all | bytes 4472832 | tf_op jit(solution)/shard_map/all_to_all | solution.py:127
  316.5 1.2 convolution_bitcast_fusion
  317.7 3.7 copy.55
  321.4 5.0 all-to-all-start.3
  326.4 2.3 copy.56
  328.7 3.9 fusion.93
  336.9 1.7 fusion.20
  338.6 41.6 %all-to-all-done.3 = f32[32,1,17472]{2,1,0:T(1,128)} async-done(((f32[32,1,17472]{2,1,0:T(1,128)}), f32[32,1,17472]{2,1,0:T(1,128)}, u32[]{:S(2)}, u32[]{:S(2)}) %all-to-all-start.3) | async-done | bytes 2236448 | tf_op jit(solution)/shard_map/all_to_all | solution.py:131
  380.2 5.1 all-to-all-start.4
  385.5 8.4 %reduce.1 = f32[32,17472]{1,0:T(8,128)} reduce(f32[32,1,17472]{2,1,0:T(1,128)} %all-to-all-done.3, f32[]{:T(128)} %constant.24), dimensions={1}, to_apply=%all_to_all.56.reduce_sub_computation | reduce | bytes 4472836 | tf_op jit(solution)/shard_map/all_to_all | solution.py:131
  393.9 2.2 reshape.146
  396.1 3.1 fusion.27
  402.8 2.3 copy.57
  405.1 33.7 %all-gather.5.cloned.1.call-done = bf16[1024,512]{0,1:T(8,128)(2,1)} async-done(((bf16[128,512]{0,1:T(8,128)(2,1)}), bf16[1024,512]{0,1:T(8,128)(2,1)}) %all-gather.5.cloned.1.call-update) | async-done | bytes 1048592 | tf_op jit(solution)/shard_map/all_gather | solution.py:157
  438.7 3.3 convolution_bitcast_fusion.2
  442.0 2.5 copy.67
  444.6 2.2 fusion.21
  446.7 2.0 copy.58
  448.8 7.0 %fusion.5 = f32[16,128,128]{1,2,0:T(8,128)S(1)} fusion(f32[16,273,128]{2,1,0:T(8,128)S(1)} %reshape.146, f32[16,256,128]{2,1,0:T(8,128)} %bitcast.250, f32[16,16,128]{2,1,0:T(8,128)S(1)} %copy-done.17, f32[273]{0:T(512)} %copy-done.23), kind=kOutput, calls=%fused_computation.18 | convolution fusion | flops 859901952 | bytes 5514308 | tf_op jit(solution)/shard_map/het,hed->htd/dot_general | solution.py:71
  455.8 1.4 fusion.10
  458.1 4.7 fusion
  462.8 72.8 %reduce-scatter.4.cloned.1.call-done = f32[16,512]{1,0:T(8,128)} async-done(((f32[512,512]{1,0:T(8,128)}), f32[16,512]{1,0:T(8,128)}) %reduce-scatter.4.cloned.1.call-update) | async-done | bytes 32784
  (100 shorter events, 25.5 us)
Async XLA Ops:
  7.2 58.6 %all-gather.3.cloned.1.call-start = ((), (), s32[]{:S(2)}) async-start(), calls=%async_computation.6 | async-start | bytes 4718592 | tf_op jit(solution)/shard_map/all_gather | solution.py:97
  9.1 61.0 %copy-start.6 = (bf16[16,8,16,128]{3,2,1,0:T(8,128)(2,1)}, bf16[16,8,16,128]{3,2,1,0:T(8,128)(2,1)S(1)}, u32[]{:S(2)}) copy-start(bf16[16,8,16,128]{3,2,1,0:T(8,128)(2,1)S(1)} %copy.71) | copy-start | bytes 1572868
  9.1 234.8 %copy-start.23 = (f32[273]{0:T(512)}, f32[273]{0:T(512)S(1)}, u32[]{:S(2)}) copy-start(f32[273]{0:T(512)S(1)} %pad.5.clone) | copy-start | bytes 3280
  70.0 1.4 copy-start.1
  70.0 3.5 copy-start.16
  77.1 16.3 %copy-start.12 = (f32[1,559104]{1,0:T(1,128)S(1)}, f32[1,559104]{1,0:T(1,128)}, u32[]{:S(2)}) copy-start(f32[1,559104]{1,0:T(1,128)} %reshape.141) | copy-start | bytes 6709252
  166.2 4.3 copy-start.21
  166.2 5.6 %copy-start.22 = (f32[128,256]{1,0:T(8,128)S(1)}, f32[128,256]{1,0:T(8,128)}, u32[]{:S(2)}) copy-start(f32[128,256]{1,0:T(8,128)} %get-tuple-element.24) | copy-start | bytes 393220
  166.2 58.2 %all-to-all-start.1 = ((f32[32,1,17472]{2,1,0:T(1,128)}), f32[32,1,17472]{2,1,0:T(1,128)S(1)}, u32[]{:S(2)}, u32[]{:S(2)}) async-start(f32[32,1,17472]{2,1,0:T(1,128)} %copy.49), calls=%async_computation.1 | async-start | bytes 4489216 | tf_op jit(solution)/shard_map/all_to_all | solution.py:117
  171.9 0.7 copy-start.13
  175.3 66.0 %copy-start.2 = (f32[16,128,128]{2,1,0:T(8,128)}, f32[16,128,128]{2,1,0:T(8,128)S(1)}, u32[]{:S(2)}) copy-start(f32[16,128,128]{2,1,0:T(8,128)S(1)} %fusion.92) | copy-start | bytes 3145732
  234.4 7.0 %copy-start.7 = (bf16[16,8,16,128]{3,2,1,0:T(8,128)(2,1)S(1)}, bf16[16,8,16,128]{3,2,1,0:T(8,128)(2,1)}, u32[]{:S(2)}) copy-start(bf16[16,8,16,128]{3,2,1,0:T(8,128)(2,1)} %copy-done.6) | copy-start | bytes 1572868
  241.3 2.1 copy-start.11
  242.7 1.0 copy-start.5
  243.4 1.6 copy-start
  243.4 1.6 copy-start.18
  321.4 58.8 %all-to-all-start.3 = ((f32[32,1,17472]{2,1,0:T(1,128)}), f32[32,1,17472]{2,1,0:T(1,128)}, u32[]{:S(2)}, u32[]{:S(2)}) async-start(f32[32,1,17472]{2,1,0:T(1,128)} %copy.55), calls=%async_computation.3 | async-start | bytes 4489216 | tf_op jit(solution)/shard_map/all_to_all | solution.py:131
  332.6 0.9 copy-start.14
  333.5 1.2 copy-start.3
  333.5 1.4 copy-start.8
  335.9 1.0 copy-start.9
  380.2 22.6 %all-to-all-start.4 = ((bf16[128,8,512]{0,2,1:T(8,128)(2,1)}), bf16[128,8,512]{0,2,1:T(8,128)(2,1)}, u32[]{:S(2)}, u32[]{:S(2)}) async-start(bf16[128,8,512]{0,2,1:T(8,128)(2,1)} %bitcast.72), calls=%async_computation.4 | async-start | bytes 2097152 | tf_op jit(solution)/shard_map/all_to_all | solution.py:94
  385.3 53.4 %all-gather.5.cloned.1.call-start = ((), (), s32[]{:S(2)}) async-start(), calls=%async_computation.7 | async-start | bytes 1179648 | tf_op jit(solution)/shard_map/all_gather | solution.py:157
  399.5 1.2 copy-start.10
  399.5 1.2 copy-start.15
  401.7 40.3 %copy-start.19 = (bf16[128,16,16]{0,2,1:T(8,128)(2,1)}, bf16[128,16,16]{0,2,1:T(8,128)(2,1)S(1)}, u32[]{:S(2)}) copy-start(bf16[128,16,16]{0,2,1:T(8,128)(2,1)S(1)} %fusion.19) | copy-start | bytes 196612
  402.4 133.2 %reduce-scatter.4.cloned.1.call-start = ((), (), s32[]{:S(2)}) async-start(), calls=%async_computation.8 | async-start | bytes 1081344
  444.5 4.2 copy-start.17
  448.8 7.0 %copy-start.4 = (f32[16,128,128]{2,1,0:T(8,128)S(1)}, f32[16,128,128]{2,1,0:T(8,128)}, u32[]{:S(2)}) copy-start(f32[16,128,128]{2,1,0:T(8,128)} %copy-done.2) | copy-start | bytes 3145732
  455.8 2.4 copy-start.20
Sparse Core Ops, SparseCore 0:
  9.8 55.8 all-gather.2
  402.6 36.1 all-gather.4
  444.7 90.8 reduce-scatter.3
